TPU v7x, 512 devices: a whole 4x4x16 slice. The times are simulated.
512 devices in a mesh: ctx: 16 (over x, z_hi), fsdp: 32 (over z_lo, y, core).
Axes of the slice: x: 4, y: 4, z: 16 (z_hi: 4, z_lo: 4; z = z_hi * 4 + z_lo), core: 2. Of those that a mesh axis runs over, the one named last changes fastest.
Arguments:
- block_pos: int32 [8, 16], P(None, 'ctx'), may hold values from 0 to 15, each once within a row
- queries: bfloat16 [32, 2048, 640], P('fsdp', 'ctx'), may hold values from -6 to 6
- keys: bfloat16 [32, 2048, 128], P('fsdp', 'ctx'), may hold values from -6 to 6
- values: bfloat16 [32, 2048, 128], P('fsdp', 'ctx'), may hold values from -12 to 12
- attention_output: bfloat16 [32, 2048, 640], P('fsdp', 'ctx'), may hold values from -6 to 6
- output_gradient: bfloat16 [32, 2048, 640], P('fsdp', 'ctx'), may hold values from -24 to 24
- log_softmax_norm: float32 [32, 5, 2048], P('fsdp', None, 'ctx'), may hold values from 6 to 9
- features: bfloat16 [8, 2048, 2560], P(None, 'ctx', 'fsdp'), may hold values from -0.119628906 to 0.119628906
Outputs:
- grad_q: bfloat16 [32, 2048, 640], P('fsdp', 'ctx')
- key_gradient: bfloat16 [32, 2048, 128], P('fsdp', 'ctx')
- value_gradient: bfloat16 [32, 2048, 128], P('fsdp', 'ctx')
- grad_wk: float32 [2560, 512], P('fsdp')
Inputs may be any that keep to these rules, and one draw needn't show every extreme that they name: Each row of block_pos holds every block place 0 to 15 once.
All inputs are finite; a program needn't handle non-finite values.
Results may differ from a plain program's by a relative error of at most 0.0058.
Values may be sent and summed in bfloat16 or wider, within the bound.
No kernel may reach another device: no remote copies, remote signals or barrier semaphores. Data moves between devices by JAX's collectives and lax.ppermute only.
A program may use at most 64 MiB of HBM per device.

v0:
```python
import jax
import jax.numpy as jnp
from jax import lax
from jax.sharding import PartitionSpec as P

QUERY_HEADS = 20
KEY_VALUE_HEADS = 4
HEAD_SIZE = 128
HEAD_GROUPS = 4


def from_behind(value, axis, steps):
    count = lax.axis_size(axis)
    pairs = [(source, (source + steps) % count) for source in range(count)]
    return lax.ppermute(value, axis, pairs)


def shortened(shard):

    def short(part):
        return part.astype(jnp.bfloat16) if part.dtype == jnp.float32 else part

    return jax.tree.map(short, shard)


def block_grads(
    heads_of_queries,
    head_gradient,
    delta_heads,
    heads_of_norm,
    block_of_keys,
    block_of_values,
    key_place,
    key_offset,
    own_place,
):
    query_rows = heads_of_queries.shape[0]
    key_rows = block_of_keys.shape[0]
    score_scale = heads_of_queries.shape[-1] ** (-0.5)
    query_pos = own_place * query_rows + lax.iota(jnp.int32, query_rows)
    key_pos = key_place[0] * query_rows + key_offset + lax.iota(jnp.int32, key_rows)
    visible = key_pos[None, :] <= query_pos[:, None]
    scores = (
        jnp.einsum(
            "tkgd,ukd->kgtu", heads_of_queries, block_of_keys, preferred_element_type=jnp.float32
        )
        * score_scale
    )
    soft_probs = jnp.where(visible, jnp.exp(scores - heads_of_norm[..., None]), 0.0)
    dprobs = jnp.einsum(
        "tkgd,ukd->kgtu", head_gradient, block_of_values, preferred_element_type=jnp.float32
    )
    dscores = (soft_probs * (dprobs - delta_heads[..., None]) * score_scale).astype(jnp.bfloat16)
    probs_low = soft_probs.astype(jnp.bfloat16)
    grad_query = jnp.einsum(
        "kgtu,ukd->tkgd", dscores, block_of_keys, preferred_element_type=jnp.float32
    )
    gradient_for_key = jnp.einsum(
        "kgtu,tkgd->ukd", dscores, heads_of_queries, preferred_element_type=jnp.float32
    )
    gradient_for_value = jnp.einsum(
        "kgtu,tkgd->ukd", probs_low, head_gradient, preferred_element_type=jnp.float32
    )
    return (grad_query, gradient_for_key, gradient_for_value)


def local(
    block_pos, queries, keys, values, attention_output, output_gradient, log_softmax_norm, features
):
    rows_per_block = queries.shape[1]
    group_size = QUERY_HEADS // KEY_VALUE_HEADS
    kv_local = keys.shape[-1] // HEAD_SIZE
    sequence_index = lax.axis_index("fsdp") // HEAD_GROUPS
    own_row = lax.dynamic_slice_in_dim(block_pos, sequence_index, 1, 0)
    own_place = own_row[0, 0]
    key_place = own_row[0, 0:1]
    heads_of_queries = queries[0].reshape(rows_per_block, kv_local, group_size, HEAD_SIZE)
    head_gradient = output_gradient[0].reshape(rows_per_block, kv_local, group_size, HEAD_SIZE)
    heads_of_output = attention_output[0].reshape(rows_per_block, kv_local, group_size, HEAD_SIZE)
    delta = jnp.sum(
        head_gradient.astype(jnp.float32) * heads_of_output.astype(jnp.float32), axis=-1
    )
    delta_heads = jnp.transpose(delta, (1, 2, 0))
    heads_of_norm = log_softmax_norm[0].reshape(kv_local, group_size, rows_per_block)
    block_of_keys = keys[0].reshape(rows_per_block, kv_local, HEAD_SIZE)
    block_of_values = values[0].reshape(rows_per_block, kv_local, HEAD_SIZE)
    cycle_length = lax.axis_size("ctx")
    zero_key_gradient = jnp.zeros((rows_per_block, kv_local, HEAD_SIZE), jnp.float32)
    zero_query_gradient = jnp.zeros((rows_per_block, kv_local, group_size, HEAD_SIZE), jnp.float32)

    def visit_rows(query_acc, blocks, grad_pair, key_offset):
        add_query, add_key, add_value = block_grads(
            heads_of_queries,
            head_gradient,
            delta_heads,
            heads_of_norm,
            blocks[0],
            blocks[1],
            blocks[2],
            key_offset,
            own_place,
        )
        return (query_acc + add_query, (grad_pair[0] + add_key, grad_pair[1] + add_value))

    def visit(query_acc, blocks, grad_pair):
        return visit_rows(query_acc, blocks, grad_pair, 0)

    def pass_grads(grad_pair):
        return from_behind(grad_pair, "ctx", 1)

    def cycle_step(step_index, cycle_state):
        query_acc, blocks, grad_pair = cycle_state
        query_acc, grad_pair = visit(query_acc, blocks, grad_pair)
        blocks = jax.tree.map(
            lambda part, own: part.astype(own.dtype),
            from_behind(shortened(blocks), "ctx", 1),
            blocks,
        )
        grad_pair = pass_grads(grad_pair)
        return (query_acc, blocks, grad_pair)

    cycle_state = (
        zero_query_gradient,
        (block_of_keys, block_of_values, key_place),
        (zero_key_gradient, zero_key_gradient),
    )
    query_acc, blocks, grad_pair = lax.fori_loop(0, cycle_length - 1, cycle_step, cycle_state)
    query_acc, grad_pair = visit(query_acc, blocks, grad_pair)
    grad_pair = pass_grads(grad_pair)
    key_gradient_sum = grad_pair[0]
    value_gradient_sum = grad_pair[1]
    grad_q = query_acc.reshape(rows_per_block, -1).astype(jnp.bfloat16)
    key_gradient = key_gradient_sum.reshape(rows_per_block, -1).astype(jnp.bfloat16)
    value_gradient = value_gradient_sum.reshape(rows_per_block, -1).astype(jnp.bfloat16)
    local_width = key_gradient.shape[-1]
    feature_cols = features.shape[-1]
    piece = lax.all_gather(key_gradient[None], "fsdp", axis=0, tiled=True)
    count = piece.shape[0]
    indices = lax.iota(jnp.int32, count)
    seq_ids = indices // HEAD_GROUPS
    group_ids = indices % HEAD_GROUPS
    chosen = jnp.take(features, seq_ids, axis=0)
    contrib = jnp.einsum("pti,ptj->pij", chosen, piece, preferred_element_type=jnp.float32)
    rounded = lax.optimization_barrier(contrib.astype(jnp.bfloat16)).astype(jnp.float32)
    placing = (group_ids[:, None] == lax.iota(jnp.int32, HEAD_GROUPS)[None, :]).astype(jnp.float32)
    summed = jnp.einsum("pij,pr->irj", rounded, placing)
    summed = summed.reshape(feature_cols, HEAD_GROUPS * local_width)
    grad_wk = lax.psum(summed, "ctx")
    return (grad_q[None], key_gradient[None], value_gradient[None], grad_wk)


def solution(mesh):
    return jax.shard_map(
        local,
        mesh=mesh,
        in_specs=(
            P(None, "ctx"),
            P("fsdp", "ctx", None),
            P("fsdp", "ctx", None),
            P("fsdp", "ctx", None),
            P("fsdp", "ctx", None),
            P("fsdp", "ctx", None),
            P("fsdp", None, "ctx"),
            P(None, "ctx", "fsdp"),
        ),
        out_specs=(
            P("fsdp", "ctx", None),
            P("fsdp", "ctx", None),
            P("fsdp", "ctx", None),
            P("fsdp", None),
        ),
        check_vma=False,
    )
```

profile of v0, /device:TPU:2, one launch (start us, length us, event | category | flops | bytes accessed | tf_op | source)
XLA Modules:
  0.0 845.0 jit_solution(10300200507523520744)
XLA Ops:
  12.6 541.2 %while.23 = (s32[]{:T(128)}, f32[128,1,5,128]{3,0,2,1:T(8,128)S(1)}, bf16[128,1,128]{2,0,1:T(8,128)(2,1)S(1)}, bf16[128,1,128]{2,0,1:T(8,128)(2,1)S(1)}, s32[1]{...) while((s32[]{:T(128)}, ...), condition=%wide.region_2.3_spmd.clone, body=%wide.region_1.2_spmd.clone.sunk | while | flops 105726208 | bytes 4103563 | solution.py:127
  12.6 9.1 %collective-permute-start = (bf16[128,1,128]{2,0,1:T(8,128)(2,1)S(1)}, bf16[128,1,128]{2,0,1:T(8,128)(2,1)S(1)}, u32[]{:S(2)}, u32[]{:S(2)}) collective-permute-start(bf16[128,1,128]{2,0,1:T(8,128)(2,1)S(1)} %copy.66), channel_id=1, source_target_pairs={{0,32},{32,64},{64,96},{96,128},{128,160},{160,192},{192,224},{224... | collective-permute-start | bytes 98312 | tf_op jit(solution)/shard_map/while/body/eval_jaxpr/ppermute | solution.py:15
  21.7 9.1 %collective-permute-start.1 = (bf16[128,1,128]{2,0,1:T(8,128)(2,1)S(1)}, bf16[128,1,128]{2,0,1:T(8,128)(2,1)S(1)}, u32[]{:S(2)}, u32[]{:S(2)}) collective-permute-start(bf16[128,1,128]{2,0,1:T(8,128)(2,1)S(1)} %copy.67), channel_id=1, source_target_pairs={{0,32},{32,64},{64,96},{96,128},{128,160},{160,192},{192,224},{224... | collective-permute-start | bytes 98312 | tf_op jit(solution)/shard_map/while/body/eval_jaxpr/ppermute | solution.py:15
  45.9 7.4 collective-permute-done.3
  57.8 8.3 collective-permute-start.1
  94.6 8.3 collective-permute-start.1
  119.1 6.7 collective-permute-done.4
  125.8 8.3 collective-permute-start
  148.5 7.0 collective-permute-start.4
  166.6 6.5 collective-permute-start.1
  180.2 6.9 collective-permute-start.3
  201.6 6.5 collective-permute-start.1
  208.6 7.9 collective-permute-start.2
  247.4 7.0 collective-permute-start.3
  254.6 8.1 collective-permute-start.4
  266.0 6.8 collective-permute-start
  297.5 7.8 collective-permute-done.4
  308.2 8.9 %collective-permute-start.1 = (bf16[128,1,128]{2,0,1:T(8,128)(2,1)S(1)}, bf16[128,1,128]{2,0,1:T(8,128)(2,1)S(1)}, u32[]{:S(2)}, u32[]{:S(2)}) collective-permute-start(bf16[128,1,128]{2,0,1:T(8,128)(2,1)S(1)} %copy.67), channel_id=1, source_target_pairs={{0,32},{32,64},{64,96},{96,128},{128,160},{160,192},{192,224},{224... | collective-permute-start | bytes 98312 | tf_op jit(solution)/shard_map/while/body/eval_jaxpr/ppermute | solution.py:15
  341.9 7.4 collective-permute-start.1
  349.8 9.7 %collective-permute-start.2 = (s32[1]{0:T(128)}, s32[1]{0:T(128)}, u32[]{:S(2)}, u32[]{:S(2)}) collective-permute-start(s32[1]{0:T(128)} %copy.68), channel_id=1, source_target_pairs={{0,32},{32,64},{64,96},{96,128},{128,160},{160,192},{192,224},{224... | collective-permute-start | bytes 20 | tf_op jit(solution)/shard_map/while/body/eval_jaxpr/ppermute | solution.py:15
  384.5 7.4 collective-permute-start.2
  415.0 7.3 collective-permute-start.1
  446.3 6.5 collective-permute-start
  476.0 6.7 collective-permute-done.4
  490.0 9.6 %collective-permute-start.2 = (s32[1]{0:T(128)}, s32[1]{0:T(128)}, u32[]{:S(2)}, u32[]{:S(2)}) collective-permute-start(s32[1]{0:T(128)} %copy.68), channel_id=1, source_target_pairs={{0,32},{32,64},{64,96},{96,128},{128,160},{160,192},{192,224},{224... | collective-permute-start | bytes 20 | tf_op jit(solution)/shard_map/while/body/eval_jaxpr/ppermute | solution.py:15
  512.0 6.8 collective-permute-done.4
  523.2 8.2 collective-permute-start.2
  532.8 9.4 %collective-permute-start.3 = (f32[128,1,128]{2,0,1:T(8,128)S(1)}, f32[128,1,128]{2,0,1:T(8,128)S(1)}, u32[]{:S(2)}, u32[]{:S(2)}) collective-permute-start(f32[128,1,128]{2,0,1:T(8,128)S(1)} %fusion.89), channel_id=1, source_target_pairs={{0,32},{32,64},{64,96},{96,128},{128,160},{160,192},{192,224},{224... | collective-permute-start | bytes 196616 | tf_op jit(solution)/shard_map/while/body/eval_jaxpr/ppermute | solution.py:15
  544.7 9.1 %collective-permute-done.4 = f32[128,1,128]{2,0,1:T(8,128)S(1)} collective-permute-done((f32[128,1,128]{2,0,1:T(8,128)S(1)}, f32[128,1,128]{2,0,1:T(8,128)S(1)}, u32[]{:S(2)}, u32[]{:S(2)}) %collective-permute-start.4) | collective-permute-done | bytes 65568 | tf_op jit(solution)/shard_map/while/body/eval_jaxpr/ppermute | solution.py:15
  557.7 8.7 %collective-permute-done.5 = bf16[128,1,128]{2,0,1:T(8,128)(2,1)S(1)} collective-permute-done((bf16[128,1,128]{2,0,1:T(8,128)(2,1)S(1)}, bf16[128,1,128]{2,0,1:T(8,128)(2,1)S(1)}, u32[]{:S(2)}, u32[]{:S(2)}) %collective-permute-start.5) | collective-permute-done | bytes 32800 | tf_op jit(solution)/shard_map/ppermute | solution.py:15
  570.1 63.8 %all-gather.3.cloned.1.call-done = bf16[4096,1,128]{2,0,1:T(8,128)(2,1)} async-done(((bf16[128,1,128]{2,0,1:T(8,128)(2,1)}), bf16[4096,1,128]{2,0,1:T(8,128)(2,1)}) %all-gather.3.cloned.1.call-update) | async-done | bytes 1048592 | tf_op jit(solution)/shard_map/all_gather | solution.py:137
  637.8 197.5 %all-reduce.2.cloned.1.call-done = f32[80,512]{1,0:T(8,128)} async-done(((f32[80,512]{1,0:T(8,128)}), f32[80,512]{1,0:T(8,128)}) %all-reduce.2.cloned.1.call-update) | async-done | bytes 163856 | tf_op jit(solution)/shard_map/psum | solution.py:148
  (331 shorter events, 331.3 us)
Async XLA Ops:
  7.2 626.7 %all-gather.3.cloned.1.call-start = ((), (), s32[]{:S(2)}) async-start(), calls=%async_computation.1 | async-start | bytes 1081344 | tf_op jit(solution)/shard_map/all_gather | solution.py:137
  12.6 33.3 %collective-permute-start = (bf16[128,1,128]{2,0,1:T(8,128)(2,1)S(1)}, bf16[128,1,128]{2,0,1:T(8,128)(2,1)S(1)}, u32[]{:S(2)}, u32[]{:S(2)}) collective-permute-start(bf16[128,1,128]{2,0,1:T(8,128)(2,1)S(1)} %copy.66), channel_id=1, source_target_pairs={{0,32},{32,64},{64,96},{96,128},{128,160},{160,192},{192,224},{224... | collective-permute-start | bytes 98312 | tf_op jit(solution)/shard_map/while/body/eval_jaxpr/ppermute | solution.py:15
  21.7 24.2 %collective-permute-start.1 = (bf16[128,1,128]{2,0,1:T(8,128)(2,1)S(1)}, bf16[128,1,128]{2,0,1:T(8,128)(2,1)S(1)}, u32[]{:S(2)}, u32[]{:S(2)}) collective-permute-start(bf16[128,1,128]{2,0,1:T(8,128)(2,1)S(1)} %copy.67), channel_id=1, source_target_pairs={{0,32},{32,64},{64,96},{96,128},{128,160},{160,192},{192,224},{224... | collective-permute-start | bytes 98312 | tf_op jit(solution)/shard_map/while/body/eval_jaxpr/ppermute | solution.py:15
  54.0 27.8 %collective-permute-start = (bf16[128,1,128]{2,0,1:T(8,128)(2,1)S(1)}, bf16[128,1,128]{2,0,1:T(8,128)(2,1)S(1)}, u32[]{:S(2)}, u32[]{:S(2)}) collective-permute-start(bf16[128,1,128]{2,0,1:T(8,128)(2,1)S(1)} %copy.66), channel_id=1, source_target_pairs={{0,32},{32,64},{64,96},{96,128},{128,160},{160,192},{192,224},{224... | collective-permute-start | bytes 98312 | tf_op jit(solution)/shard_map/while/body/eval_jaxpr/ppermute | solution.py:15
  57.8 24.0 %collective-permute-start.1 = (bf16[128,1,128]{2,0,1:T(8,128)(2,1)S(1)}, bf16[128,1,128]{2,0,1:T(8,128)(2,1)S(1)}, u32[]{:S(2)}, u32[]{:S(2)}) collective-permute-start(bf16[128,1,128]{2,0,1:T(8,128)(2,1)S(1)} %copy.67), channel_id=1, source_target_pairs={{0,32},{32,64},{64,96},{96,128},{128,160},{160,192},{192,224},{224... | collective-permute-start | bytes 98312 | tf_op jit(solution)/shard_map/while/body/eval_jaxpr/ppermute | solution.py:15
  89.6 28.9 %collective-permute-start = (bf16[128,1,128]{2,0,1:T(8,128)(2,1)S(1)}, bf16[128,1,128]{2,0,1:T(8,128)(2,1)S(1)}, u32[]{:S(2)}, u32[]{:S(2)}) collective-permute-start(bf16[128,1,128]{2,0,1:T(8,128)(2,1)S(1)} %copy.66), channel_id=1, source_target_pairs={{0,32},{32,64},{64,96},{96,128},{128,160},{160,192},{192,224},{224... | collective-permute-start | bytes 98312 | tf_op jit(solution)/shard_map/while/body/eval_jaxpr/ppermute | solution.py:15
  94.6 23.9 %collective-permute-start.1 = (bf16[128,1,128]{2,0,1:T(8,128)(2,1)S(1)}, bf16[128,1,128]{2,0,1:T(8,128)(2,1)S(1)}, u32[]{:S(2)}, u32[]{:S(2)}) collective-permute-start(bf16[128,1,128]{2,0,1:T(8,128)(2,1)S(1)} %copy.67), channel_id=1, source_target_pairs={{0,32},{32,64},{64,96},{96,128},{128,160},{160,192},{192,224},{224... | collective-permute-start | bytes 98312 | tf_op jit(solution)/shard_map/while/body/eval_jaxpr/ppermute | solution.py:15
  125.8 30.1 %collective-permute-start = (bf16[128,1,128]{2,0,1:T(8,128)(2,1)S(1)}, bf16[128,1,128]{2,0,1:T(8,128)(2,1)S(1)}, u32[]{:S(2)}, u32[]{:S(2)}) collective-permute-start(bf16[128,1,128]{2,0,1:T(8,128)(2,1)S(1)} %copy.66), channel_id=1, source_target_pairs={{0,32},{32,64},{64,96},{96,128},{128,160},{160,192},{192,224},{224... | collective-permute-start | bytes 98312 | tf_op jit(solution)/shard_map/while/body/eval_jaxpr/ppermute | solution.py:15
  134.1 21.8 %collective-permute-start.1 = (bf16[128,1,128]{2,0,1:T(8,128)(2,1)S(1)}, bf16[128,1,128]{2,0,1:T(8,128)(2,1)S(1)}, u32[]{:S(2)}, u32[]{:S(2)}) collective-permute-start(bf16[128,1,128]{2,0,1:T(8,128)(2,1)S(1)} %copy.67), channel_id=1, source_target_pairs={{0,32},{32,64},{64,96},{96,128},{128,160},{160,192},{192,224},{224... | collective-permute-start | bytes 98312 | tf_op jit(solution)/shard_map/while/body/eval_jaxpr/ppermute | solution.py:15
  160.6 30.4 %collective-permute-start = (bf16[128,1,128]{2,0,1:T(8,128)(2,1)S(1)}, bf16[128,1,128]{2,0,1:T(8,128)(2,1)S(1)}, u32[]{:S(2)}, u32[]{:S(2)}) collective-permute-start(bf16[128,1,128]{2,0,1:T(8,128)(2,1)S(1)} %copy.66), channel_id=1, source_target_pairs={{0,32},{32,64},{64,96},{96,128},{128,160},{160,192},{192,224},{224... | collective-permute-start | bytes 98312 | tf_op jit(solution)/shard_map/while/body/eval_jaxpr/ppermute | solution.py:15
  166.6 24.4 %collective-permute-start.1 = (bf16[128,1,128]{2,0,1:T(8,128)(2,1)S(1)}, bf16[128,1,128]{2,0,1:T(8,128)(2,1)S(1)}, u32[]{:S(2)}, u32[]{:S(2)}) collective-permute-start(bf16[128,1,128]{2,0,1:T(8,128)(2,1)S(1)} %copy.67), channel_id=1, source_target_pairs={{0,32},{32,64},{64,96},{96,128},{128,160},{160,192},{192,224},{224... | collective-permute-start | bytes 98312 | tf_op jit(solution)/shard_map/while/body/eval_jaxpr/ppermute | solution.py:15
  198.3 27.4 %collective-permute-start = (bf16[128,1,128]{2,0,1:T(8,128)(2,1)S(1)}, bf16[128,1,128]{2,0,1:T(8,128)(2,1)S(1)}, u32[]{:S(2)}, u32[]{:S(2)}) collective-permute-start(bf16[128,1,128]{2,0,1:T(8,128)(2,1)S(1)} %copy.66), channel_id=1, source_target_pairs={{0,32},{32,64},{64,96},{96,128},{128,160},{160,192},{192,224},{224... | collective-permute-start | bytes 98312 | tf_op jit(solution)/shard_map/while/body/eval_jaxpr/ppermute | solution.py:15
  201.6 24.1 %collective-permute-start.1 = (bf16[128,1,128]{2,0,1:T(8,128)(2,1)S(1)}, bf16[128,1,128]{2,0,1:T(8,128)(2,1)S(1)}, u32[]{:S(2)}, u32[]{:S(2)}) collective-permute-start(bf16[128,1,128]{2,0,1:T(8,128)(2,1)S(1)} %copy.67), channel_id=1, source_target_pairs={{0,32},{32,64},{64,96},{96,128},{128,160},{160,192},{192,224},{224... | collective-permute-start | bytes 98312 | tf_op jit(solution)/shard_map/while/body/eval_jaxpr/ppermute | solution.py:15
  233.6 29.4 %collective-permute-start = (bf16[128,1,128]{2,0,1:T(8,128)(2,1)S(1)}, bf16[128,1,128]{2,0,1:T(8,128)(2,1)S(1)}, u32[]{:S(2)}, u32[]{:S(2)}) collective-permute-start(bf16[128,1,128]{2,0,1:T(8,128)(2,1)S(1)} %copy.66), channel_id=1, source_target_pairs={{0,32},{32,64},{64,96},{96,128},{128,160},{160,192},{192,224},{224... | collective-permute-start | bytes 98312 | tf_op jit(solution)/shard_map/while/body/eval_jaxpr/ppermute | solution.py:15
  236.2 26.9 %collective-permute-start.1 = (bf16[128,1,128]{2,0,1:T(8,128)(2,1)S(1)}, bf16[128,1,128]{2,0,1:T(8,128)(2,1)S(1)}, u32[]{:S(2)}, u32[]{:S(2)}) collective-permute-start(bf16[128,1,128]{2,0,1:T(8,128)(2,1)S(1)} %copy.67), channel_id=1, source_target_pairs={{0,32},{32,64},{64,96},{96,128},{128,160},{160,192},{192,224},{224... | collective-permute-start | bytes 98312 | tf_op jit(solution)/shard_map/while/body/eval_jaxpr/ppermute | solution.py:15
  266.0 31.5 %collective-permute-start = (bf16[128,1,128]{2,0,1:T(8,128)(2,1)S(1)}, bf16[128,1,128]{2,0,1:T(8,128)(2,1)S(1)}, u32[]{:S(2)}, u32[]{:S(2)}) collective-permute-start(bf16[128,1,128]{2,0,1:T(8,128)(2,1)S(1)} %copy.66), channel_id=1, source_target_pairs={{0,32},{32,64},{64,96},{96,128},{128,160},{160,192},{192,224},{224... | collective-permute-start | bytes 98312 | tf_op jit(solution)/shard_map/while/body/eval_jaxpr/ppermute | solution.py:15
  272.8 24.7 %collective-permute-start.1 = (bf16[128,1,128]{2,0,1:T(8,128)(2,1)S(1)}, bf16[128,1,128]{2,0,1:T(8,128)(2,1)S(1)}, u32[]{:S(2)}, u32[]{:S(2)}) collective-permute-start(bf16[128,1,128]{2,0,1:T(8,128)(2,1)S(1)} %copy.67), channel_id=1, source_target_pairs={{0,32},{32,64},{64,96},{96,128},{128,160},{160,192},{192,224},{224... | collective-permute-start | bytes 98312 | tf_op jit(solution)/shard_map/while/body/eval_jaxpr/ppermute | solution.py:15
  305.3 25.5 %collective-permute-start = (bf16[128,1,128]{2,0,1:T(8,128)(2,1)S(1)}, bf16[128,1,128]{2,0,1:T(8,128)(2,1)S(1)}, u32[]{:S(2)}, u32[]{:S(2)}) collective-permute-start(bf16[128,1,128]{2,0,1:T(8,128)(2,1)S(1)} %copy.66), channel_id=1, source_target_pairs={{0,32},{32,64},{64,96},{96,128},{128,160},{160,192},{192,224},{224... | collective-permute-start | bytes 98312 | tf_op jit(solution)/shard_map/while/body/eval_jaxpr/ppermute | solution.py:15
  308.2 22.6 %collective-permute-start.1 = (bf16[128,1,128]{2,0,1:T(8,128)(2,1)S(1)}, bf16[128,1,128]{2,0,1:T(8,128)(2,1)S(1)}, u32[]{:S(2)}, u32[]{:S(2)}) collective-permute-start(bf16[128,1,128]{2,0,1:T(8,128)(2,1)S(1)} %copy.67), channel_id=1, source_target_pairs={{0,32},{32,64},{64,96},{96,128},{128,160},{160,192},{192,224},{224... | collective-permute-start | bytes 98312 | tf_op jit(solution)/shard_map/while/body/eval_jaxpr/ppermute | solution.py:15
  340.0 27.1 %collective-permute-start = (bf16[128,1,128]{2,0,1:T(8,128)(2,1)S(1)}, bf16[128,1,128]{2,0,1:T(8,128)(2,1)S(1)}, u32[]{:S(2)}, u32[]{:S(2)}) collective-permute-start(bf16[128,1,128]{2,0,1:T(8,128)(2,1)S(1)} %copy.66), channel_id=1, source_target_pairs={{0,32},{32,64},{64,96},{96,128},{128,160},{160,192},{192,224},{224... | collective-permute-start | bytes 98312 | tf_op jit(solution)/shard_map/while/body/eval_jaxpr/ppermute | solution.py:15
  341.9 25.1 %collective-permute-start.1 = (bf16[128,1,128]{2,0,1:T(8,128)(2,1)S(1)}, bf16[128,1,128]{2,0,1:T(8,128)(2,1)S(1)}, u32[]{:S(2)}, u32[]{:S(2)}) collective-permute-start(bf16[128,1,128]{2,0,1:T(8,128)(2,1)S(1)} %copy.67), channel_id=1, source_target_pairs={{0,32},{32,64},{64,96},{96,128},{128,160},{160,192},{192,224},{224... | collective-permute-start | bytes 98312 | tf_op jit(solution)/shard_map/while/body/eval_jaxpr/ppermute | solution.py:15
  375.7 29.3 %collective-permute-start = (bf16[128,1,128]{2,0,1:T(8,128)(2,1)S(1)}, bf16[128,1,128]{2,0,1:T(8,128)(2,1)S(1)}, u32[]{:S(2)}, u32[]{:S(2)}) collective-permute-start(bf16[128,1,128]{2,0,1:T(8,128)(2,1)S(1)} %copy.66), channel_id=1, source_target_pairs={{0,32},{32,64},{64,96},{96,128},{128,160},{160,192},{192,224},{224... | collective-permute-start | bytes 98312 | tf_op jit(solution)/shard_map/while/body/eval_jaxpr/ppermute | solution.py:15
  378.6 26.4 %collective-permute-start.1 = (bf16[128,1,128]{2,0,1:T(8,128)(2,1)S(1)}, bf16[128,1,128]{2,0,1:T(8,128)(2,1)S(1)}, u32[]{:S(2)}, u32[]{:S(2)}) collective-permute-start(bf16[128,1,128]{2,0,1:T(8,128)(2,1)S(1)} %copy.67), channel_id=1, source_target_pairs={{0,32},{32,64},{64,96},{96,128},{128,160},{160,192},{192,224},{224... | collective-permute-start | bytes 98312 | tf_op jit(solution)/shard_map/while/body/eval_jaxpr/ppermute | solution.py:15
  410.8 30.8 %collective-permute-start = (bf16[128,1,128]{2,0,1:T(8,128)(2,1)S(1)}, bf16[128,1,128]{2,0,1:T(8,128)(2,1)S(1)}, u32[]{:S(2)}, u32[]{:S(2)}) collective-permute-start(bf16[128,1,128]{2,0,1:T(8,128)(2,1)S(1)} %copy.66), channel_id=1, source_target_pairs={{0,32},{32,64},{64,96},{96,128},{128,160},{160,192},{192,224},{224... | collective-permute-start | bytes 98312 | tf_op jit(solution)/shard_map/while/body/eval_jaxpr/ppermute | solution.py:15
  415.0 26.7 %collective-permute-start.1 = (bf16[128,1,128]{2,0,1:T(8,128)(2,1)S(1)}, bf16[128,1,128]{2,0,1:T(8,128)(2,1)S(1)}, u32[]{:S(2)}, u32[]{:S(2)}) collective-permute-start(bf16[128,1,128]{2,0,1:T(8,128)(2,1)S(1)} %copy.67), channel_id=1, source_target_pairs={{0,32},{32,64},{64,96},{96,128},{128,160},{160,192},{192,224},{224... | collective-permute-start | bytes 98312 | tf_op jit(solution)/shard_map/while/body/eval_jaxpr/ppermute | solution.py:15
  446.3 26.8 %collective-permute-start = (bf16[128,1,128]{2,0,1:T(8,128)(2,1)S(1)}, bf16[128,1,128]{2,0,1:T(8,128)(2,1)S(1)}, u32[]{:S(2)}, u32[]{:S(2)}) collective-permute-start(bf16[128,1,128]{2,0,1:T(8,128)(2,1)S(1)} %copy.66), channel_id=1, source_target_pairs={{0,32},{32,64},{64,96},{96,128},{128,160},{160,192},{192,224},{224... | collective-permute-start | bytes 98312 | tf_op jit(solution)/shard_map/while/body/eval_jaxpr/ppermute | solution.py:15
  482.7 25.7 %collective-permute-start = (bf16[128,1,128]{2,0,1:T(8,128)(2,1)S(1)}, bf16[128,1,128]{2,0,1:T(8,128)(2,1)S(1)}, u32[]{:S(2)}, u32[]{:S(2)}) collective-permute-start(bf16[128,1,128]{2,0,1:T(8,128)(2,1)S(1)} %copy.66), channel_id=1, source_target_pairs={{0,32},{32,64},{64,96},{96,128},{128,160},{160,192},{192,224},{224... | collective-permute-start | bytes 98312 | tf_op jit(solution)/shard_map/while/body/eval_jaxpr/ppermute | solution.py:15
  484.6 23.8 %collective-permute-start.1 = (bf16[128,1,128]{2,0,1:T(8,128)(2,1)S(1)}, bf16[128,1,128]{2,0,1:T(8,128)(2,1)S(1)}, u32[]{:S(2)}, u32[]{:S(2)}) collective-permute-start(bf16[128,1,128]{2,0,1:T(8,128)(2,1)S(1)} %copy.67), channel_id=1, source_target_pairs={{0,32},{32,64},{64,96},{96,128},{128,160},{160,192},{192,224},{224... | collective-permute-start | bytes 98312 | tf_op jit(solution)/shard_map/while/body/eval_jaxpr/ppermute | solution.py:15
  518.8 25.9 %collective-permute-start = (bf16[128,1,128]{2,0,1:T(8,128)(2,1)S(1)}, bf16[128,1,128]{2,0,1:T(8,128)(2,1)S(1)}, u32[]{:S(2)}, u32[]{:S(2)}) collective-permute-start(bf16[128,1,128]{2,0,1:T(8,128)(2,1)S(1)} %copy.66), channel_id=1, source_target_pairs={{0,32},{32,64},{64,96},{96,128},{128,160},{160,192},{192,224},{224... | collective-permute-start | bytes 98312 | tf_op jit(solution)/shard_map/while/body/eval_jaxpr/ppermute | solution.py:15
  520.7 24.0 %collective-permute-start.1 = (bf16[128,1,128]{2,0,1:T(8,128)(2,1)S(1)}, bf16[128,1,128]{2,0,1:T(8,128)(2,1)S(1)}, u32[]{:S(2)}, u32[]{:S(2)}) collective-permute-start(bf16[128,1,128]{2,0,1:T(8,128)(2,1)S(1)} %copy.67), channel_id=1, source_target_pairs={{0,32},{32,64},{64,96},{96,128},{128,160},{160,192},{192,224},{224... | collective-permute-start | bytes 98312 | tf_op jit(solution)/shard_map/while/body/eval_jaxpr/ppermute | solution.py:15
  567.0 268.3 %all-reduce.2.cloned.1.call-start = ((), (), s32[]{:S(2)}) async-start(), calls=%async_computation | async-start | bytes 327680 | tf_op jit(solution)/shard_map/psum | solution.py:148
  567.3 70.6 %collective-permute-start.6 = (bf16[128,1,128]{2,0,1:T(8,128)(2,1)S(1)}, bf16[128,1,128]{2,0,1:T(8,128)(2,1)S(1)}, u32[]{:S(2)}, u32[]{:S(2)}) collective-permute-start(bf16[128,1,128]{2,0,1:T(8,128)(2,1)S(1)} %fusion.33), channel_id=1, source_target_pairs={{0,32},{32,64},{64,96},{96,128},{128,160},{160,192},{192,224},{224... | collective-permute-start | bytes 98312 | tf_op jit(solution)/shard_map/ppermute | solution.py:15
  (57 other events, 1423.9 us)
Sparse Core Ops, SparseCore 0:
  567.1 66.7 all-gather.2
  637.4 197.8 all-reduce.1
where the time goes:
time: 848 us; the launch traced here: 845 us
  starting transfers between devices  396 us (47%)
  waiting for transfers between devices  381 us (45%)
  matrix products  19.6 us (2%)
  between operations  14.8 us (2%)
  other arithmetic  12.4 us (1%)
  local copies, waits for them, and re-layouts  10.7 us (1%)
  loops' own time  10.2 us (1%)
    ppermute x77, starting transfers between devices, from_behind(): return lax.ppermute(value, axis, pairs)  396 us
    psum x1, waiting for transfers between devices, local(): grad_wk = lax.psum(summed, 'ctx')  197 us
    ppermute x77, waiting for transfers between devices, from_behind(): return lax.ppermute(value, axis, pairs)  120 us
    all_gather x1, waiting for transfers between devices, local(): piece = lax.all_gather(key_gradient[None], 'fsdp', axis=0, tiled=True)  63.8 us
  transfers between devices with their start and end apart: 79, of which 30 were waited for; matrix products, arithmetic and copies ran while one was open for 4% of the time, Pallas kernels for 0%

commit v1 on v0

--- a/solution.py
+++ b/solution.py
@@ -145,7 +145,7 @@
     placing = (group_ids[:, None] == lax.iota(jnp.int32, HEAD_GROUPS)[None, :]).astype(jnp.float32)
     summed = jnp.einsum("pij,pr->irj", rounded, placing)
     summed = summed.reshape(feature_cols, HEAD_GROUPS * local_width)
-    grad_wk = lax.psum(summed, "ctx")
+    grad_wk = jnp.sum(lax.all_gather(summed, "ctx"), axis=0)
     return (grad_q[None], key_gradient[None], value_gradient[None], grad_wk)
 
 

time: 848 us -> 756 us (0.89)
  the two profiles are of different devices: /device:TPU:2 before, /device:TPU:1 now
where the time goes in v1:
time: 756 us; the launch traced here: 753 us
  waiting for transfers between devices  347 us (46%)
  starting transfers between devices  336 us (44%)
  matrix products  19.6 us (3%)
  other arithmetic  15.7 us (2%)
  between operations  14.8 us (2%)
  loops' own time  10.3 us (1%)
  local copies, waits for them, and re-layouts  10.2 us (1%)
    ppermute x77, starting transfers between devices, from_behind(): return lax.ppermute(value, axis, pairs)  335 us
    ppermute x77, waiting for transfers between devices, from_behind(): return lax.ppermute(value, axis, pairs)  148 us
    all_gather x1, waiting for transfers between devices, local(): piece = lax.all_gather(key_gradient[None], 'fsdp', axis=0, tiled=True)  106 us
    all_gather x1, waiting for transfers between devices, local(): grad_wk = jnp.sum(lax.all_gather(summed, 'ctx'), axis=0)  93.4 us
  transfers between devices with their start and end apart: 79, of which 30 were waited for; matrix products, arithmetic and copies ran while one was open for 4% of the time, Pallas kernels for 0%

profile of v1, /device:TPU:1, one launch (start us, length us, event | category | flops | bytes accessed | tf_op | source)
XLA Modules:
  0.0 753.3 jit_solution(16213953933261884513)
XLA Ops:
  14.4 500.8 %while.23 = (s32[]{:T(128)}, f32[128,1,5,128]{3,0,2,1:T(8,128)S(1)}, bf16[128,1,128]{2,0,1:T(8,128)(2,1)S(1)}, bf16[128,1,128]{2,0,1:T(8,128)(2,1)S(1)}, s32[1]{...) while((s32[]{:T(128)}, ...), condition=%wide.region_2.3_spmd.clone, body=%wide.region_1.2_spmd.clone.sunk | while | flops 105726208 | bytes 4103563 | solution.py:127
  14.4 9.6 %collective-permute-start = (bf16[128,1,128]{2,0,1:T(8,128)(2,1)S(1)}, bf16[128,1,128]{2,0,1:T(8,128)(2,1)S(1)}, u32[]{:S(2)}, u32[]{:S(2)}) collective-permute-start(bf16[128,1,128]{2,0,1:T(8,128)(2,1)S(1)} %copy.80), channel_id=1, source_target_pairs={{0,32},{32,64},{64,96},{96,128},{128,160},{160,192},{192,224},{224... | collective-permute-start | bytes 98312 | tf_op jit(solution)/shard_map/while/body/eval_jaxpr/ppermute | solution.py:15
  24.1 8.8 %collective-permute-start.1 = (bf16[128,1,128]{2,0,1:T(8,128)(2,1)S(1)}, bf16[128,1,128]{2,0,1:T(8,128)(2,1)S(1)}, u32[]{:S(2)}, u32[]{:S(2)}) collective-permute-start(bf16[128,1,128]{2,0,1:T(8,128)(2,1)S(1)} %copy.81), channel_id=1, source_target_pairs={{0,32},{32,64},{64,96},{96,128},{128,160},{160,192},{192,224},{224... | collective-permute-start | bytes 98312 | tf_op jit(solution)/shard_map/while/body/eval_jaxpr/ppermute | solution.py:15
  57.0 8.9 %collective-permute-start.1 = (bf16[128,1,128]{2,0,1:T(8,128)(2,1)S(1)}, bf16[128,1,128]{2,0,1:T(8,128)(2,1)S(1)}, u32[]{:S(2)}, u32[]{:S(2)}) collective-permute-start(bf16[128,1,128]{2,0,1:T(8,128)(2,1)S(1)} %copy.81), channel_id=1, source_target_pairs={{0,32},{32,64},{64,96},{96,128},{128,160},{160,192},{192,224},{224... | collective-permute-start | bytes 98312 | tf_op jit(solution)/shard_map/while/body/eval_jaxpr/ppermute | solution.py:15
  90.3 7.0 collective-permute-start.1
  114.1 6.8 collective-permute-done.4
  133.6 7.9 %collective-permute-start.3 = (f32[128,1,128]{2,0,1:T(8,128)S(1)}, f32[128,1,128]{2,0,1:T(8,128)S(1)}, u32[]{:S(2)}, u32[]{:S(2)}) collective-permute-start(f32[128,1,128]{2,0,1:T(8,128)S(1)} %fusion.87), channel_id=1, source_target_pairs={{0,32},{32,64},{64,96},{96,128},{128,160},{160,192},{192,224},{224... | collective-permute-start | bytes 196616 | tf_op jit(solution)/shard_map/while/body/eval_jaxpr/ppermute | solution.py:15
  145.1 9.7 %collective-permute-done.4 = f32[128,1,128]{2,0,1:T(8,128)S(1)} collective-permute-done((f32[128,1,128]{2,0,1:T(8,128)S(1)}, f32[128,1,128]{2,0,1:T(8,128)S(1)}, u32[]{:S(2)}, u32[]{:S(2)}) %collective-permute-start.4) | collective-permute-done | bytes 65568 | tf_op jit(solution)/shard_map/while/body/eval_jaxpr/ppermute | solution.py:15
  164.7 9.5 %collective-permute-start.3 = (f32[128,1,128]{2,0,1:T(8,128)S(1)}, f32[128,1,128]{2,0,1:T(8,128)S(1)}, u32[]{:S(2)}, u32[]{:S(2)}) collective-permute-start(f32[128,1,128]{2,0,1:T(8,128)S(1)} %fusion.87), channel_id=1, source_target_pairs={{0,32},{32,64},{64,96},{96,128},{128,160},{160,192},{192,224},{224... | collective-permute-start | bytes 196616 | tf_op jit(solution)/shard_map/while/body/eval_jaxpr/ppermute | solution.py:15
  177.7 8.8 %collective-permute-done.4 = f32[128,1,128]{2,0,1:T(8,128)S(1)} collective-permute-done((f32[128,1,128]{2,0,1:T(8,128)S(1)}, f32[128,1,128]{2,0,1:T(8,128)S(1)}, u32[]{:S(2)}, u32[]{:S(2)}) %collective-permute-start.4) | collective-permute-done | bytes 65568 | tf_op jit(solution)/shard_map/while/body/eval_jaxpr/ppermute | solution.py:15
  200.0 8.0 %collective-permute-start.3 = (f32[128,1,128]{2,0,1:T(8,128)S(1)}, f32[128,1,128]{2,0,1:T(8,128)S(1)}, u32[]{:S(2)}, u32[]{:S(2)}) collective-permute-start(f32[128,1,128]{2,0,1:T(8,128)S(1)} %fusion.87), channel_id=1, source_target_pairs={{0,32},{32,64},{64,96},{96,128},{128,160},{160,192},{192,224},{224... | collective-permute-start | bytes 196616 | tf_op jit(solution)/shard_map/while/body/eval_jaxpr/ppermute | solution.py:15
  211.4 11.2 %collective-permute-done.4 = f32[128,1,128]{2,0,1:T(8,128)S(1)} collective-permute-done((f32[128,1,128]{2,0,1:T(8,128)S(1)}, f32[128,1,128]{2,0,1:T(8,128)S(1)}, u32[]{:S(2)}, u32[]{:S(2)}) %collective-permute-start.4) | collective-permute-done | bytes 65568 | tf_op jit(solution)/shard_map/while/body/eval_jaxpr/ppermute | solution.py:15
  231.4 10.2 %collective-permute-start.3 = (f32[128,1,128]{2,0,1:T(8,128)S(1)}, f32[128,1,128]{2,0,1:T(8,128)S(1)}, u32[]{:S(2)}, u32[]{:S(2)}) collective-permute-start(f32[128,1,128]{2,0,1:T(8,128)S(1)} %fusion.87), channel_id=1, source_target_pairs={{0,32},{32,64},{64,96},{96,128},{128,160},{160,192},{192,224},{224... | collective-permute-start | bytes 196616 | tf_op jit(solution)/shard_map/while/body/eval_jaxpr/ppermute | solution.py:15
  244.0 8.8 %collective-permute-done.4 = f32[128,1,128]{2,0,1:T(8,128)S(1)} collective-permute-done((f32[128,1,128]{2,0,1:T(8,128)S(1)}, f32[128,1,128]{2,0,1:T(8,128)S(1)}, u32[]{:S(2)}, u32[]{:S(2)}) %collective-permute-start.4) | collective-permute-done | bytes 65568 | tf_op jit(solution)/shard_map/while/body/eval_jaxpr/ppermute | solution.py:15
  257.2 10.7 %collective-permute-start.2 = (s32[1]{0:T(128)}, s32[1]{0:T(128)}, u32[]{:S(2)}, u32[]{:S(2)}) collective-permute-start(s32[1]{0:T(128)} %copy.82), channel_id=1, source_target_pairs={{0,32},{32,64},{64,96},{96,128},{128,160},{160,192},{192,224},{224... | collective-permute-start | bytes 20 | tf_op jit(solution)/shard_map/while/body/eval_jaxpr/ppermute | solution.py:15
  269.3 9.1 %collective-permute-start.3 = (f32[128,1,128]{2,0,1:T(8,128)S(1)}, f32[128,1,128]{2,0,1:T(8,128)S(1)}, u32[]{:S(2)}, u32[]{:S(2)}) collective-permute-start(f32[128,1,128]{2,0,1:T(8,128)S(1)} %fusion.87), channel_id=1, source_target_pairs={{0,32},{32,64},{64,96},{96,128},{128,160},{160,192},{192,224},{224... | collective-permute-start | bytes 196616 | tf_op jit(solution)/shard_map/while/body/eval_jaxpr/ppermute | solution.py:15
  281.6 12.4 %collective-permute-done.4 = f32[128,1,128]{2,0,1:T(8,128)S(1)} collective-permute-done((f32[128,1,128]{2,0,1:T(8,128)S(1)}, f32[128,1,128]{2,0,1:T(8,128)S(1)}, u32[]{:S(2)}, u32[]{:S(2)}) %collective-permute-start.4) | collective-permute-done | bytes 65568 | tf_op jit(solution)/shard_map/while/body/eval_jaxpr/ppermute | solution.py:15
  323.0 11.5 %collective-permute-start.2 = (s32[1]{0:T(128)}, s32[1]{0:T(128)}, u32[]{:S(2)}, u32[]{:S(2)}) collective-permute-start(s32[1]{0:T(128)} %copy.82), channel_id=1, source_target_pairs={{0,32},{32,64},{64,96},{96,128},{128,160},{160,192},{192,224},{224... | collective-permute-start | bytes 20 | tf_op jit(solution)/shard_map/while/body/eval_jaxpr/ppermute | solution.py:15
  335.8 8.6 %collective-permute-start.3 = (f32[128,1,128]{2,0,1:T(8,128)S(1)}, f32[128,1,128]{2,0,1:T(8,128)S(1)}, u32[]{:S(2)}, u32[]{:S(2)}) collective-permute-start(f32[128,1,128]{2,0,1:T(8,128)S(1)} %fusion.87), channel_id=1, source_target_pairs={{0,32},{32,64},{64,96},{96,128},{128,160},{160,192},{192,224},{224... | collective-permute-start | bytes 196616 | tf_op jit(solution)/shard_map/while/body/eval_jaxpr/ppermute | solution.py:15
  348.6 7.9 %collective-permute-done.4 = f32[128,1,128]{2,0,1:T(8,128)S(1)} collective-permute-done((f32[128,1,128]{2,0,1:T(8,128)S(1)}, f32[128,1,128]{2,0,1:T(8,128)S(1)}, u32[]{:S(2)}, u32[]{:S(2)}) %collective-permute-start.4) | collective-permute-done | bytes 65568 | tf_op jit(solution)/shard_map/while/body/eval_jaxpr/ppermute | solution.py:15
  384.5 10.3 %collective-permute-start.1 = (bf16[128,1,128]{2,0,1:T(8,128)(2,1)S(1)}, bf16[128,1,128]{2,0,1:T(8,128)(2,1)S(1)}, u32[]{:S(2)}, u32[]{:S(2)}) collective-permute-start(bf16[128,1,128]{2,0,1:T(8,128)(2,1)S(1)} %copy.81), channel_id=1, source_target_pairs={{0,32},{32,64},{64,96},{96,128},{128,160},{160,192},{192,224},{224... | collective-permute-start | bytes 98312 | tf_op jit(solution)/shard_map/while/body/eval_jaxpr/ppermute | solution.py:15
  395.4 10.3 %collective-permute-start.2 = (s32[1]{0:T(128)}, s32[1]{0:T(128)}, u32[]{:S(2)}, u32[]{:S(2)}) collective-permute-start(s32[1]{0:T(128)} %copy.82), channel_id=1, source_target_pairs={{0,32},{32,64},{64,96},{96,128},{128,160},{160,192},{192,224},{224... | collective-permute-start | bytes 20 | tf_op jit(solution)/shard_map/while/body/eval_jaxpr/ppermute | solution.py:15
  407.1 9.1 %collective-permute-start.3 = (f32[128,1,128]{2,0,1:T(8,128)S(1)}, f32[128,1,128]{2,0,1:T(8,128)S(1)}, u32[]{:S(2)}, u32[]{:S(2)}) collective-permute-start(f32[128,1,128]{2,0,1:T(8,128)S(1)} %fusion.87), channel_id=1, source_target_pairs={{0,32},{32,64},{64,96},{96,128},{128,160},{160,192},{192,224},{224... | collective-permute-start | bytes 196616 | tf_op jit(solution)/shard_map/while/body/eval_jaxpr/ppermute | solution.py:15
  418.6 10.7 %collective-permute-done.4 = f32[128,1,128]{2,0,1:T(8,128)S(1)} collective-permute-done((f32[128,1,128]{2,0,1:T(8,128)S(1)}, f32[128,1,128]{2,0,1:T(8,128)S(1)}, u32[]{:S(2)}, u32[]{:S(2)}) %collective-permute-start.4) | collective-permute-done | bytes 65568 | tf_op jit(solution)/shard_map/while/body/eval_jaxpr/ppermute | solution.py:15
  457.2 8.6 %collective-permute-start.2 = (s32[1]{0:T(128)}, s32[1]{0:T(128)}, u32[]{:S(2)}, u32[]{:S(2)}) collective-permute-start(s32[1]{0:T(128)} %copy.82), channel_id=1, source_target_pairs={{0,32},{32,64},{64,96},{96,128},{128,160},{160,192},{192,224},{224... | collective-permute-start | bytes 20 | tf_op jit(solution)/shard_map/while/body/eval_jaxpr/ppermute | solution.py:15
  467.3 7.4 collective-permute-start.3
  478.9 8.0 %collective-permute-done.4 = f32[128,1,128]{2,0,1:T(8,128)S(1)} collective-permute-done((f32[128,1,128]{2,0,1:T(8,128)S(1)}, f32[128,1,128]{2,0,1:T(8,128)S(1)}, u32[]{:S(2)}, u32[]{:S(2)}) %collective-permute-start.4) | collective-permute-done | bytes 65568 | tf_op jit(solution)/shard_map/while/body/eval_jaxpr/ppermute | solution.py:15
  495.3 8.4 %collective-permute-start.3 = (f32[128,1,128]{2,0,1:T(8,128)S(1)}, f32[128,1,128]{2,0,1:T(8,128)S(1)}, u32[]{:S(2)}, u32[]{:S(2)}) collective-permute-start(f32[128,1,128]{2,0,1:T(8,128)S(1)} %fusion.87), channel_id=1, source_target_pairs={{0,32},{32,64},{64,96},{96,128},{128,160},{160,192},{192,224},{224... | collective-permute-start | bytes 196616 | tf_op jit(solution)/shard_map/while/body/eval_jaxpr/ppermute | solution.py:15
  517.2 7.1 collective-permute-start.5
  529.4 106.0 %all-gather.6.cloned.1.call-done = bf16[4096,1,128]{2,0,1:T(8,128)(2,1)} async-done(((bf16[128,1,128]{2,0,1:T(8,128)(2,1)}), bf16[4096,1,128]{2,0,1:T(8,128)(2,1)}) %all-gather.6.cloned.1.call-update) | async-done | bytes 1048592 | tf_op jit(solution)/shard_map/all_gather | solution.py:137
  638.3 7.4 collective-permute-start.6
  649.2 93.4 %all-gather.4.cloned.1.call-done = f32[16,80,512]{2,1,0:T(8,128)} async-done(((f32[1,80,512]{2,1,0:T(8,128)}), f32[16,80,512]{2,1,0:T(8,128)}) %all-gather.4.cloned.1.call-update) | async-done | bytes 2621456 | tf_op jit(solution)/shard_map/all_gather | solution.py:148
  (318 shorter events, 266.2 us)
Async XLA Ops:
  7.2 628.2 %all-gather.6.cloned.1.call-start = ((), (), s32[]{:S(2)}) async-start(), calls=%async_computation.1 | async-start | bytes 1081344 | tf_op jit(solution)/shard_map/all_gather | solution.py:137
  14.4 32.2 %collective-permute-start = (bf16[128,1,128]{2,0,1:T(8,128)(2,1)S(1)}, bf16[128,1,128]{2,0,1:T(8,128)(2,1)S(1)}, u32[]{:S(2)}, u32[]{:S(2)}) collective-permute-start(bf16[128,1,128]{2,0,1:T(8,128)(2,1)S(1)} %copy.80), channel_id=1, source_target_pairs={{0,32},{32,64},{64,96},{96,128},{128,160},{160,192},{192,224},{224... | collective-permute-start | bytes 98312 | tf_op jit(solution)/shard_map/while/body/eval_jaxpr/ppermute | solution.py:15
  24.1 22.5 %collective-permute-start.1 = (bf16[128,1,128]{2,0,1:T(8,128)(2,1)S(1)}, bf16[128,1,128]{2,0,1:T(8,128)(2,1)S(1)}, u32[]{:S(2)}, u32[]{:S(2)}) collective-permute-start(bf16[128,1,128]{2,0,1:T(8,128)(2,1)S(1)} %copy.81), channel_id=1, source_target_pairs={{0,32},{32,64},{64,96},{96,128},{128,160},{160,192},{192,224},{224... | collective-permute-start | bytes 98312 | tf_op jit(solution)/shard_map/while/body/eval_jaxpr/ppermute | solution.py:15
  54.8 24.8 %collective-permute-start = (bf16[128,1,128]{2,0,1:T(8,128)(2,1)S(1)}, bf16[128,1,128]{2,0,1:T(8,128)(2,1)S(1)}, u32[]{:S(2)}, u32[]{:S(2)}) collective-permute-start(bf16[128,1,128]{2,0,1:T(8,128)(2,1)S(1)} %copy.80), channel_id=1, source_target_pairs={{0,32},{32,64},{64,96},{96,128},{128,160},{160,192},{192,224},{224... | collective-permute-start | bytes 98312 | tf_op jit(solution)/shard_map/while/body/eval_jaxpr/ppermute | solution.py:15
  57.0 22.5 %collective-permute-start.1 = (bf16[128,1,128]{2,0,1:T(8,128)(2,1)S(1)}, bf16[128,1,128]{2,0,1:T(8,128)(2,1)S(1)}, u32[]{:S(2)}, u32[]{:S(2)}) collective-permute-start(bf16[128,1,128]{2,0,1:T(8,128)(2,1)S(1)} %copy.81), channel_id=1, source_target_pairs={{0,32},{32,64},{64,96},{96,128},{128,160},{160,192},{192,224},{224... | collective-permute-start | bytes 98312 | tf_op jit(solution)/shard_map/while/body/eval_jaxpr/ppermute | solution.py:15
  88.4 23.7 %collective-permute-start = (bf16[128,1,128]{2,0,1:T(8,128)(2,1)S(1)}, bf16[128,1,128]{2,0,1:T(8,128)(2,1)S(1)}, u32[]{:S(2)}, u32[]{:S(2)}) collective-permute-start(bf16[128,1,128]{2,0,1:T(8,128)(2,1)S(1)} %copy.80), channel_id=1, source_target_pairs={{0,32},{32,64},{64,96},{96,128},{128,160},{160,192},{192,224},{224... | collective-permute-start | bytes 98312 | tf_op jit(solution)/shard_map/while/body/eval_jaxpr/ppermute | solution.py:15
  90.3 21.8 %collective-permute-start.1 = (bf16[128,1,128]{2,0,1:T(8,128)(2,1)S(1)}, bf16[128,1,128]{2,0,1:T(8,128)(2,1)S(1)}, u32[]{:S(2)}, u32[]{:S(2)}) collective-permute-start(bf16[128,1,128]{2,0,1:T(8,128)(2,1)S(1)} %copy.81), channel_id=1, source_target_pairs={{0,32},{32,64},{64,96},{96,128},{128,160},{160,192},{192,224},{224... | collective-permute-start | bytes 98312 | tf_op jit(solution)/shard_map/while/body/eval_jaxpr/ppermute | solution.py:15
  120.9 23.0 %collective-permute-start = (bf16[128,1,128]{2,0,1:T(8,128)(2,1)S(1)}, bf16[128,1,128]{2,0,1:T(8,128)(2,1)S(1)}, u32[]{:S(2)}, u32[]{:S(2)}) collective-permute-start(bf16[128,1,128]{2,0,1:T(8,128)(2,1)S(1)} %copy.80), channel_id=1, source_target_pairs={{0,32},{32,64},{64,96},{96,128},{128,160},{160,192},{192,224},{224... | collective-permute-start | bytes 98312 | tf_op jit(solution)/shard_map/while/body/eval_jaxpr/ppermute | solution.py:15
  122.8 21.1 %collective-permute-start.1 = (bf16[128,1,128]{2,0,1:T(8,128)(2,1)S(1)}, bf16[128,1,128]{2,0,1:T(8,128)(2,1)S(1)}, u32[]{:S(2)}, u32[]{:S(2)}) collective-permute-start(bf16[128,1,128]{2,0,1:T(8,128)(2,1)S(1)} %copy.81), channel_id=1, source_target_pairs={{0,32},{32,64},{64,96},{96,128},{128,160},{160,192},{192,224},{224... | collective-permute-start | bytes 98312 | tf_op jit(solution)/shard_map/while/body/eval_jaxpr/ppermute | solution.py:15
  154.9 22.8 %collective-permute-start = (bf16[128,1,128]{2,0,1:T(8,128)(2,1)S(1)}, bf16[128,1,128]{2,0,1:T(8,128)(2,1)S(1)}, u32[]{:S(2)}, u32[]{:S(2)}) collective-permute-start(bf16[128,1,128]{2,0,1:T(8,128)(2,1)S(1)} %copy.80), channel_id=1, source_target_pairs={{0,32},{32,64},{64,96},{96,128},{128,160},{160,192},{192,224},{224... | collective-permute-start | bytes 98312 | tf_op jit(solution)/shard_map/while/body/eval_jaxpr/ppermute | solution.py:15
  156.8 20.9 %collective-permute-start.1 = (bf16[128,1,128]{2,0,1:T(8,128)(2,1)S(1)}, bf16[128,1,128]{2,0,1:T(8,128)(2,1)S(1)}, u32[]{:S(2)}, u32[]{:S(2)}) collective-permute-start(bf16[128,1,128]{2,0,1:T(8,128)(2,1)S(1)} %copy.81), channel_id=1, source_target_pairs={{0,32},{32,64},{64,96},{96,128},{128,160},{160,192},{192,224},{224... | collective-permute-start | bytes 98312 | tf_op jit(solution)/shard_map/while/body/eval_jaxpr/ppermute | solution.py:15
  159.9 17.8 %collective-permute-start.2 = (s32[1]{0:T(128)}, s32[1]{0:T(128)}, u32[]{:S(2)}, u32[]{:S(2)}) collective-permute-start(s32[1]{0:T(128)} %copy.82), channel_id=1, source_target_pairs={{0,32},{32,64},{64,96},{96,128},{128,160},{160,192},{192,224},{224... | collective-permute-start | bytes 20 | tf_op jit(solution)/shard_map/while/body/eval_jaxpr/ppermute | solution.py:15
  186.5 23.9 %collective-permute-start = (bf16[128,1,128]{2,0,1:T(8,128)(2,1)S(1)}, bf16[128,1,128]{2,0,1:T(8,128)(2,1)S(1)}, u32[]{:S(2)}, u32[]{:S(2)}) collective-permute-start(bf16[128,1,128]{2,0,1:T(8,128)(2,1)S(1)} %copy.80), channel_id=1, source_target_pairs={{0,32},{32,64},{64,96},{96,128},{128,160},{160,192},{192,224},{224... | collective-permute-start | bytes 98312 | tf_op jit(solution)/shard_map/while/body/eval_jaxpr/ppermute | solution.py:15
  188.5 21.9 %collective-permute-start.1 = (bf16[128,1,128]{2,0,1:T(8,128)(2,1)S(1)}, bf16[128,1,128]{2,0,1:T(8,128)(2,1)S(1)}, u32[]{:S(2)}, u32[]{:S(2)}) collective-permute-start(bf16[128,1,128]{2,0,1:T(8,128)(2,1)S(1)} %copy.81), channel_id=1, source_target_pairs={{0,32},{32,64},{64,96},{96,128},{128,160},{160,192},{192,224},{224... | collective-permute-start | bytes 98312 | tf_op jit(solution)/shard_map/while/body/eval_jaxpr/ppermute | solution.py:15
  222.6 21.4 %collective-permute-start = (bf16[128,1,128]{2,0,1:T(8,128)(2,1)S(1)}, bf16[128,1,128]{2,0,1:T(8,128)(2,1)S(1)}, u32[]{:S(2)}, u32[]{:S(2)}) collective-permute-start(bf16[128,1,128]{2,0,1:T(8,128)(2,1)S(1)} %copy.80), channel_id=1, source_target_pairs={{0,32},{32,64},{64,96},{96,128},{128,160},{160,192},{192,224},{224... | collective-permute-start | bytes 98312 | tf_op jit(solution)/shard_map/while/body/eval_jaxpr/ppermute | solution.py:15
  224.5 19.5 %collective-permute-start.1 = (bf16[128,1,128]{2,0,1:T(8,128)(2,1)S(1)}, bf16[128,1,128]{2,0,1:T(8,128)(2,1)S(1)}, u32[]{:S(2)}, u32[]{:S(2)}) collective-permute-start(bf16[128,1,128]{2,0,1:T(8,128)(2,1)S(1)} %copy.81), channel_id=1, source_target_pairs={{0,32},{32,64},{64,96},{96,128},{128,160},{160,192},{192,224},{224... | collective-permute-start | bytes 98312 | tf_op jit(solution)/shard_map/while/body/eval_jaxpr/ppermute | solution.py:15
  252.8 28.1 %collective-permute-start = (bf16[128,1,128]{2,0,1:T(8,128)(2,1)S(1)}, bf16[128,1,128]{2,0,1:T(8,128)(2,1)S(1)}, u32[]{:S(2)}, u32[]{:S(2)}) collective-permute-start(bf16[128,1,128]{2,0,1:T(8,128)(2,1)S(1)} %copy.80), channel_id=1, source_target_pairs={{0,32},{32,64},{64,96},{96,128},{128,160},{160,192},{192,224},{224... | collective-permute-start | bytes 98312 | tf_op jit(solution)/shard_map/while/body/eval_jaxpr/ppermute | solution.py:15
  254.7 26.2 %collective-permute-start.1 = (bf16[128,1,128]{2,0,1:T(8,128)(2,1)S(1)}, bf16[128,1,128]{2,0,1:T(8,128)(2,1)S(1)}, u32[]{:S(2)}, u32[]{:S(2)}) collective-permute-start(bf16[128,1,128]{2,0,1:T(8,128)(2,1)S(1)} %copy.81), channel_id=1, source_target_pairs={{0,32},{32,64},{64,96},{96,128},{128,160},{160,192},{192,224},{224... | collective-permute-start | bytes 98312 | tf_op jit(solution)/shard_map/while/body/eval_jaxpr/ppermute | solution.py:15
  257.2 23.6 %collective-permute-start.2 = (s32[1]{0:T(128)}, s32[1]{0:T(128)}, u32[]{:S(2)}, u32[]{:S(2)}) collective-permute-start(s32[1]{0:T(128)} %copy.82), channel_id=1, source_target_pairs={{0,32},{32,64},{64,96},{96,128},{128,160},{160,192},{192,224},{224... | collective-permute-start | bytes 20 | tf_op jit(solution)/shard_map/while/body/eval_jaxpr/ppermute | solution.py:15
  318.2 30.3 %collective-permute-start = (bf16[128,1,128]{2,0,1:T(8,128)(2,1)S(1)}, bf16[128,1,128]{2,0,1:T(8,128)(2,1)S(1)}, u32[]{:S(2)}, u32[]{:S(2)}) collective-permute-start(bf16[128,1,128]{2,0,1:T(8,128)(2,1)S(1)} %copy.80), channel_id=1, source_target_pairs={{0,32},{32,64},{64,96},{96,128},{128,160},{160,192},{192,224},{224... | collective-permute-start | bytes 98312 | tf_op jit(solution)/shard_map/while/body/eval_jaxpr/ppermute | solution.py:15
  320.1 28.4 %collective-permute-start.1 = (bf16[128,1,128]{2,0,1:T(8,128)(2,1)S(1)}, bf16[128,1,128]{2,0,1:T(8,128)(2,1)S(1)}, u32[]{:S(2)}, u32[]{:S(2)}) collective-permute-start(bf16[128,1,128]{2,0,1:T(8,128)(2,1)S(1)} %copy.81), channel_id=1, source_target_pairs={{0,32},{32,64},{64,96},{96,128},{128,160},{160,192},{192,224},{224... | collective-permute-start | bytes 98312 | tf_op jit(solution)/shard_map/while/body/eval_jaxpr/ppermute | solution.py:15
  323.0 25.5 %collective-permute-start.2 = (s32[1]{0:T(128)}, s32[1]{0:T(128)}, u32[]{:S(2)}, u32[]{:S(2)}) collective-permute-start(s32[1]{0:T(128)} %copy.82), channel_id=1, source_target_pairs={{0,32},{32,64},{64,96},{96,128},{128,160},{160,192},{192,224},{224... | collective-permute-start | bytes 20 | tf_op jit(solution)/shard_map/while/body/eval_jaxpr/ppermute | solution.py:15
  382.6 36.0 %collective-permute-start = (bf16[128,1,128]{2,0,1:T(8,128)(2,1)S(1)}, bf16[128,1,128]{2,0,1:T(8,128)(2,1)S(1)}, u32[]{:S(2)}, u32[]{:S(2)}) collective-permute-start(bf16[128,1,128]{2,0,1:T(8,128)(2,1)S(1)} %copy.80), channel_id=1, source_target_pairs={{0,32},{32,64},{64,96},{96,128},{128,160},{160,192},{192,224},{224... | collective-permute-start | bytes 98312 | tf_op jit(solution)/shard_map/while/body/eval_jaxpr/ppermute | solution.py:15
  384.5 34.1 %collective-permute-start.1 = (bf16[128,1,128]{2,0,1:T(8,128)(2,1)S(1)}, bf16[128,1,128]{2,0,1:T(8,128)(2,1)S(1)}, u32[]{:S(2)}, u32[]{:S(2)}) collective-permute-start(bf16[128,1,128]{2,0,1:T(8,128)(2,1)S(1)} %copy.81), channel_id=1, source_target_pairs={{0,32},{32,64},{64,96},{96,128},{128,160},{160,192},{192,224},{224... | collective-permute-start | bytes 98312 | tf_op jit(solution)/shard_map/while/body/eval_jaxpr/ppermute | solution.py:15
  395.4 23.2 %collective-permute-start.2 = (s32[1]{0:T(128)}, s32[1]{0:T(128)}, u32[]{:S(2)}, u32[]{:S(2)}) collective-permute-start(s32[1]{0:T(128)} %copy.82), channel_id=1, source_target_pairs={{0,32},{32,64},{64,96},{96,128},{128,160},{160,192},{192,224},{224... | collective-permute-start | bytes 20 | tf_op jit(solution)/shard_map/while/body/eval_jaxpr/ppermute | solution.py:15
  451.9 25.2 %collective-permute-start = (bf16[128,1,128]{2,0,1:T(8,128)(2,1)S(1)}, bf16[128,1,128]{2,0,1:T(8,128)(2,1)S(1)}, u32[]{:S(2)}, u32[]{:S(2)}) collective-permute-start(bf16[128,1,128]{2,0,1:T(8,128)(2,1)S(1)} %copy.80), channel_id=1, source_target_pairs={{0,32},{32,64},{64,96},{96,128},{128,160},{160,192},{192,224},{224... | collective-permute-start | bytes 98312 | tf_op jit(solution)/shard_map/while/body/eval_jaxpr/ppermute | solution.py:15
  453.8 23.3 %collective-permute-start.1 = (bf16[128,1,128]{2,0,1:T(8,128)(2,1)S(1)}, bf16[128,1,128]{2,0,1:T(8,128)(2,1)S(1)}, u32[]{:S(2)}, u32[]{:S(2)}) collective-permute-start(bf16[128,1,128]{2,0,1:T(8,128)(2,1)S(1)} %copy.81), channel_id=1, source_target_pairs={{0,32},{32,64},{64,96},{96,128},{128,160},{160,192},{192,224},{224... | collective-permute-start | bytes 98312 | tf_op jit(solution)/shard_map/while/body/eval_jaxpr/ppermute | solution.py:15
  457.2 19.8 %collective-permute-start.2 = (s32[1]{0:T(128)}, s32[1]{0:T(128)}, u32[]{:S(2)}, u32[]{:S(2)}) collective-permute-start(s32[1]{0:T(128)} %copy.82), channel_id=1, source_target_pairs={{0,32},{32,64},{64,96},{96,128},{128,160},{160,192},{192,224},{224... | collective-permute-start | bytes 20 | tf_op jit(solution)/shard_map/while/body/eval_jaxpr/ppermute | solution.py:15
  486.9 22.7 %collective-permute-start = (bf16[128,1,128]{2,0,1:T(8,128)(2,1)S(1)}, bf16[128,1,128]{2,0,1:T(8,128)(2,1)S(1)}, u32[]{:S(2)}, u32[]{:S(2)}) collective-permute-start(bf16[128,1,128]{2,0,1:T(8,128)(2,1)S(1)} %copy.80), channel_id=1, source_target_pairs={{0,32},{32,64},{64,96},{96,128},{128,160},{160,192},{192,224},{224... | collective-permute-start | bytes 98312 | tf_op jit(solution)/shard_map/while/body/eval_jaxpr/ppermute | solution.py:15
  488.8 20.8 %collective-permute-start.1 = (bf16[128,1,128]{2,0,1:T(8,128)(2,1)S(1)}, bf16[128,1,128]{2,0,1:T(8,128)(2,1)S(1)}, u32[]{:S(2)}, u32[]{:S(2)}) collective-permute-start(bf16[128,1,128]{2,0,1:T(8,128)(2,1)S(1)} %copy.81), channel_id=1, source_target_pairs={{0,32},{32,64},{64,96},{96,128},{128,160},{160,192},{192,224},{224... | collective-permute-start | bytes 98312 | tf_op jit(solution)/shard_map/while/body/eval_jaxpr/ppermute | solution.py:15
  491.3 18.3 %collective-permute-start.2 = (s32[1]{0:T(128)}, s32[1]{0:T(128)}, u32[]{:S(2)}, u32[]{:S(2)}) collective-permute-start(s32[1]{0:T(128)} %copy.82), channel_id=1, source_target_pairs={{0,32},{32,64},{64,96},{96,128},{128,160},{160,192},{192,224},{224... | collective-permute-start | bytes 20 | tf_op jit(solution)/shard_map/while/body/eval_jaxpr/ppermute | solution.py:15
  528.6 214.0 %all-gather.4.cloned.1.call-start = ((), (), s32[]{:S(2)}) async-start(), calls=%async_computation | async-start | bytes 2785280 | tf_op jit(solution)/shard_map/all_gather | solution.py:148
  (50 other events, 1226.2 us)
Sparse Core Ops, SparseCore 0:
  528.7 106.6 all-gather.5
  639.0 103.5 all-gather.3
